TPU v7x, 32 devices: a whole 2x2x4 slice. The times are simulated.
32 devices in a mesh: ka: 8 (over z, y), col: 4 (over x, core).
Axes of the slice: x: 2, y: 2, z: 4, core: 2. Of those that a mesh axis runs over, the one named last changes fastest.
Arguments:
- amps: bfloat16 [16, 256, 192], P('ka', 'col'), may hold values from -6 to 6
- isdf_coeffs: bfloat16 [16, 2048, 256], P('ka', 'col'), may hold values from -0.375 to 0.375
- w_screen: bfloat16 [16, 2048, 2048], P(None, 'ka', 'col'), as said below
- energies: float32 [16, 256], P('ka', 'col'), may hold values from 0.5 to 3
- qsel: int32 [2], replicated, may hold values from 0 to 15
- partner: int32 [2, 16], replicated, may hold values from 0 to 15, each once within a row
Outputs:
- applied: float32 [16, 256, 192], P('ka', 'col')
Inputs may be any that keep to these rules, and one draw needn't show every extreme that they name: Each row of partner is a permutation of the 16 k points. `w_screen`: each of the 16 matrices is symmetric.
All inputs are finite; a program needn't handle non-finite values.
Results may differ from a plain program's by a relative error of at most 0.013.
Values may be sent and summed in bfloat16 or wider, within the bound.
A program may use at most 64 MiB of HBM per device.

v0:
```python
import jax
import jax.numpy as jnp
from jax import lax
from jax.sharding import PartitionSpec as P


def body(amps, isdf_coeffs, w_screen, energies, qsel, partner):
    k_local = amps.shape[0]
    vectors = amps.shape[2]
    offset_base = lax.axis_index("ka") * k_local
    owned = offset_base + jnp.arange(k_local, dtype=jnp.int32)
    wanted = jnp.take(partner, owned, axis=1).reshape(-1)
    everyone = lax.all_gather(amps, "ka", axis=0, tiled=True)
    picked = jnp.take(everyone, wanted, axis=0)
    partners = lax.all_gather(picked, "col", axis=1, tiled=True)
    partners = partners.reshape(2, k_local, partners.shape[1], vectors)
    densities = jnp.einsum(
        "kms,qkse->qmke", isdf_coeffs, partners, preferred_element_type=jnp.float32
    )
    width = densities.shape[1]
    densities = densities.astype(jnp.bfloat16).reshape(2, width, k_local * vectors)
    slabs = jnp.take(w_screen, qsel, axis=0)
    partials = jnp.einsum(
        "qrm,qmx->qrx",
        lax.all_gather(slabs, "ka", axis=1, tiled=True),
        densities,
        preferred_element_type=jnp.float32,
    )
    screened = lax.psum_scatter(
        partials.astype(jnp.bfloat16), "col", scatter_dimension=1, tiled=True
    ).astype(jnp.float32)
    screened = screened.astype(jnp.bfloat16).reshape(2, width, k_local, vectors)
    projected = jnp.einsum(
        "kms,qmke->kse", isdf_coeffs, screened, preferred_element_type=jnp.float32
    )
    summed = lax.psum_scatter(
        projected.astype(jnp.bfloat16), "col", scatter_dimension=1, tiled=True
    ).astype(jnp.float32)
    return summed + energies[:, :, None] * amps.astype(jnp.float32)


def solution(mesh):
    placed = (
        P("ka", "col", None),
        P("ka", "col", None),
        P(None, "ka", "col"),
        P("ka", "col"),
        P(),
        P(),
    )
    return jax.shard_map(
        body, mesh=mesh, in_specs=placed, out_specs=P("ka", "col", None), check_vma=False
    )
```

profile of v0, /device:TPU:0, one launch (start us, length us, event | category | flops | bytes accessed | tf_op | source)
XLA Modules:
  0.0 176.6 jit_solution(11480643661953069329)
XLA Ops:
  6.5 0.7 compare_select_fusion.4
  7.3 0.7 compare_and_fusion.2
  7.9 2.8 %gather_fusion = bf16[2,256,512]{2,1,0:T(8,128)(2,1)S(1)} fusion(bf16[16,256,512]{2,1,0:T(8,128)(2,1)} %param.8, s32[1024]{0:T(1024)S(1)} %pad_clamp_fusion.2), kind=kCustom, calls=%fused_computation | custom fusion | bytes 1048584 | tf_op jit(solution)/shard_map/jit(_take)/gather | solution.py:22
  10.7 0.9 broadcast_select_fusion
  11.6 0.0 all-gather.2.cloned.1.call-update
  11.7 0.0 reduce-scatter.2.cloned.1.call-start
  11.7 0.8 copy.53
  12.5 0.6 gather_fusion.1
  13.1 0.1 select_bitcast_fusion
  13.1 0.1 copy.54
  13.2 0.1 select_n.71
  13.3 0.1 select_n.69
  13.4 35.6 %all_gather.10 = bf16[16,64,192]{2,1,0:T(8,128)(2,1)S(1)} all-gather(bf16[2,64,192]{2,1,0:T(8,128)(2,1)} %param.6), channel_id=1, replica_groups=mesh['ka'=8,'col'=4] {'ka'}, dimensions={0}, use_global_device_ids=true | all-gather | bytes 442368 | tf_op jit(solution)/shard_map/all_gather | solution.py:13
  49.0 0.6 gather_fusion.2
  49.6 0.1 broadcast_select_fusion.1
  49.7 7.1 %all_gather.11 = bf16[4,256,192]{2,1,0:T(8,128)(2,1)S(1)} all-gather(bf16[4,64,192]{2,1,0:T(8,128)(2,1)S(1)} %broadcast_select_fusion.1), channel_id=1, replica_groups=mesh['ka'=8,'col'=4] {'col'}, dimensions={1}, use_global_device_ids=true | all-gather | bytes 491520 | tf_op jit(solution)/shard_map/all_gather | solution.py:15
  56.8 0.5 fusion
  57.3 0.1 copy.58
  57.4 33.2 %all-gather.2.cloned.1.call-done = bf16[2,2048,512]{2,1,0:T(8,128)(2,1)} async-done(((bf16[2,256,512]{2,1,0:T(8,128)(2,1)}), bf16[2,2048,512]{2,1,0:T(8,128)(2,1)}) %all-gather.2.cloned.1.call-update) | async-done | bytes 4194320 | tf_op jit(solution)/shard_map/all_gather | solution.py:25
  90.6 6.2 %convolution_convert_fusion = bf16[2,2048,384]{2,1,0:T(8,128)(2,1)} fusion(bf16[2,2048,512]{2,1,0:T(8,128)(2,1)} %all-gather.2.cloned.1.call-done, bf16[2,512,384]{1,2,0:T(8,128)(2,1)S(1)} %bitcast.25), kind=kOutput, calls=%fused_computation.3 | convolution fusion | flops 1612185600 | bytes 8126464 | tf_op jit(solution)/shard_map/qrm,qmx->qrx/dot_general | solution.py:23
  96.8 0.0 reduce-scatter.2.cloned.1.call-update
  96.9 0.0 all-reduce.3.cloned.1.call-start
  96.9 36.5 %reduce-scatter.2.cloned.1.call-done = bf16[2,512,384]{2,1,0:T(8,128)(2,1)} async-done(((bf16[2,2048,384]{2,1,0:T(8,128)(2,1)}), bf16[2,512,384]{2,1,0:T(8,128)(2,1)}) %reduce-scatter.2.cloned.1.call-update) | async-done | bytes 786448 | tf_op jit(solution)/shard_map/reduce_scatter | solution.py:29
  133.4 1.2 convert_reduce_fusion
  134.7 0.2 copy.60
  134.9 0.3 fusion.1
  135.1 0.9 copy.61
  136.0 0.0 all-reduce.3.cloned.1.call-update
  136.0 0.6 dynamic-slice
  137.3 31.2 %all-reduce.3.cloned.1.call-done = bf16[2,256,192]{2,0,1:T(2,128)(2,1)} async-done(((bf16[2,256,192]{2,0,1:T(2,128)(2,1)}), bf16[2,256,192]{2,0,1:T(2,128)(2,1)}) %all-reduce.3.cloned.1.call-update) | async-done | bytes 196624
  168.5 0.9 constant_dynamic-slice_fusion
  169.4 0.7 multiply_add_fusion
  (16 shorter events, 0.1 us)
Async XLA Ops:
  6.5 50.3 %copy-start = (bf16[2,512,256]{2,1,0:T(8,128)(2,1)S(1)}, bf16[2,512,256]{2,1,0:T(8,128)(2,1)}, u32[]{:S(2)}) copy-start(bf16[2,512,256]{2,1,0:T(8,128)(2,1)} %param.7) | copy-start | bytes 1572868
  6.5 84.1 %all-gather.2.cloned.1.call-start = ((), (), s32[]{:S(2)}) async-start(), calls=%async_computation.1 | async-start | bytes 4718592 | tf_op jit(solution)/shard_map/all_gather | solution.py:25
  11.7 121.7 %reduce-scatter.2.cloned.1.call-start = ((), (), s32[]{:S(2)}) async-start(), calls=%async_computation.2 | async-start | bytes 3932160 | tf_op jit(solution)/shard_map/reduce_scatter | solution.py:29
  96.8 39.2 %copy-start.3 = (u32[32]{0:T(128)S(1)}, u32[32]{0:T(128)}, u32[]{:S(2)}) copy-start(u32[32]{0:T(128)} %constant.56) | copy-start | bytes 388
  96.8 72.5 %copy-start.1 = (bf16[2,64,192]{2,1,0:T(8,128)(2,1)S(1)}, bf16[2,64,192]{2,1,0:T(8,128)(2,1)}, u32[]{:S(2)}) copy-start(bf16[2,64,192]{2,1,0:T(8,128)(2,1)} %param.6) | copy-start | bytes 147460
  96.8 72.5 %copy-start.2 = (f32[2,64]{1,0:T(2,128)S(1)}, f32[2,64]{1,0:T(2,128)}, u32[]{:S(2)}) copy-start(f32[2,64]{1,0:T(2,128)} %param.9) | copy-start | bytes 1540
  96.9 71.6 %all-reduce.3.cloned.1.call-start = ((), (), s32[]{:S(2)}) async-start(), calls=%async_computation.3 | async-start | bytes 524288
Sparse Core Ops, SparseCore 0:
  11.8 78.7 all-gather.1
  97.0 36.3 reduce-scatter.1
  136.2 32.2 all-reduce.2
where the time goes:
time: 177 us
  waiting for transfers between devices  101 us (57%)
  blocking collectives  42.7 us (24%)
  between operations  13.9 us (8%)
  local copies, waits for them, and re-layouts  7.5 us (4%)
  matrix products  6.98 us (4%)
  other arithmetic  4.51 us (3%)
    reduce_scatter x1, waiting for transfers between devices, body(): lax.psum_scatter(partials.astype(jnp.bfloat16), 'col', scatter_dimension=...  36.5 us
    all_gather x1, blocking collectives, body(): everyone = lax.all_gather(amps, 'ka', axis=0, tiled=True)  35.6 us
    all_gather x1, waiting for transfers between devices, body(): lax.all_gather(slabs, 'ka', axis=1, tiled=True)  33.2 us
    unnamed x4, waiting for transfers between devices  31.2 us
    all_gather x1, blocking collectives, body(): partners = lax.all_gather(picked, 'col', axis=1, tiled=True)  7.1 us
    dot_general x1, matrix products, body(): jnp.einsum('qrm,qmx->qrx', lax.all_gather(slabs, 'ka', axis=1, tiled=True...  6.23 us
  transfers between devices with their start and end apart: 3, of which 3 were waited for; matrix products, arithmetic and copies ran while one was open for 2% of the time, Pallas kernels for 0%

commit v1 on v0

--- a/solution.py
+++ b/solution.py
@@ -2,6 +2,30 @@
 import jax.numpy as jnp
 from jax import lax
 from jax.sharding import PartitionSpec as P
+
+
+def work_both_ways(shard, axis, dim, work, out_dim):
+    size, place, rows = (lax.axis_size(axis), lax.axis_index(axis), shard.shape[dim])
+    upward = [(i, (i + 1) % size) for i in range(size)]
+    behind = [(b, a) for a, b in upward]
+    lower, upper = (lax.ppermute(shard, axis, upward), lax.ppermute(shard, axis, behind))
+    made = work(shard, place * rows)
+    length = made.shape[out_dim]
+    out = jnp.zeros((*made.shape[:out_dim], size * length, *made.shape[out_dim + 1 :]), made.dtype)
+
+    def put(out, made, owner):
+        return lax.dynamic_update_slice_in_dim(out, made, owner * length, axis=out_dim)
+
+    out = put(out, made, place)
+    for step in range(1, size // 2 + 1):
+        below, above = ((place - step) % size, (place + step) % size)
+        carried = (lower, upper)
+        if step < size // 2:
+            lower, upper = (lax.ppermute(lower, axis, upward), lax.ppermute(upper, axis, behind))
+        out = put(out, work(carried[0], below * rows), below)
+        if 2 * step < size:
+            out = put(out, work(carried[1], above * rows), above)
+    return out
 
 
 def body(amps, isdf_coeffs, w_screen, energies, qsel, partner):
@@ -20,11 +44,14 @@
     width = densities.shape[1]
     densities = densities.astype(jnp.bfloat16).reshape(2, width, k_local * vectors)
     slabs = jnp.take(w_screen, qsel, axis=0)
-    partials = jnp.einsum(
-        "qrm,qmx->qrx",
-        lax.all_gather(slabs, "ka", axis=1, tiled=True),
-        densities,
-        preferred_element_type=jnp.float32,
+    partials = work_both_ways(
+        slabs,
+        "ka",
+        1,
+        lambda own_block, offset: jnp.einsum(
+            "qrm,qmx->qrx", own_block, densities, preferred_element_type=jnp.float32
+        ),
+        1,
     )
     screened = lax.psum_scatter(
         partials.astype(jnp.bfloat16), "col", scatter_dimension=1, tiled=True

time: 177 us -> 220 us (1.24)
  starting transfers between devices: 0.09 us -> 18.5 us
  blocking collectives: 42.7 us -> 53 us
  waiting for transfers between devices: 101 us -> 111 us
  matrix products: 6.98 us -> 10.4 us
    ppermute x0 -> x7, waiting for transfers between devices: none -> 44.1 us  [the longest x3 44 us: work_both_ways(): lax.ppermute(lower, axis, upward)]
    all_gather x1 -> x0, waiting for transfers between devices: 33.2 us -> none  [body(): lax.all_gather(slabs, 'ka', axis=1, tiled=True)]
    ppermute x0 -> x7, starting transfers between devices: none -> 18.5 us  [the longest x2 7.15 us: work_both_ways(): lax.ppermute(upper, axis, behind)]
    all_gather x1, blocking collectives: 35.6 us -> 45.8 us  [body(): everyone = lax.all_gather(amps, 'ka', axis=0, tiled=True)]
    dot_general x1 -> x8, matrix products: 6.23 us -> 9.6 us  [body(): jnp.einsum('qrm,qmx->qrx', own_block, densities, preferred_element_type=j...]
    unnamed x4 -> x3, waiting for transfers between devices: 31.2 us -> 31.2 us
  transfers between devices with their start and end apart: 3 -> 9, of which waited for: 3 -> 5; matrix products, arithmetic and copies ran while one was open for 2% -> 6% of each run, Pallas kernels for 0% -> 0%
where the time goes in v1:
time: 220 us
  waiting for transfers between devices  111 us (50%)
  blocking collectives  53 us (24%)
  starting transfers between devices  18.5 us (8%)
  between operations  14.2 us (6%)
  matrix products  10.4 us (5%)
  local copies, waits for them, and re-layouts  9.4 us (4%)
  other arithmetic  3.68 us (2%)
    all_gather x1, blocking collectives, body(): everyone = lax.all_gather(amps, 'ka', axis=0, tiled=True)  45.8 us
    ppermute x3, waiting for transfers between devices, work_both_ways(): lax.ppermute(lower, axis, upward)  44 us
    reduce_scatter x1, waiting for transfers between devices, body(): lax.psum_scatter(partials.astype(jnp.bfloat16), 'col', scatter_dimension=...  35.8 us
    unnamed x3, waiting for transfers between devices  31.2 us
    dot_general x8, matrix products, body(): jnp.einsum('qrm,qmx->qrx', own_block, densities, preferred_element_type=j...  9.6 us
    all_gather x1, blocking collectives, body(): partners = lax.all_gather(picked, 'col', axis=1, tiled=True)  7.17 us
    ppermute x2, starting transfers between devices, work_both_ways(): lax.ppermute(upper, axis, behind)  7.15 us
    ppermute x3, starting transfers between devices, work_both_ways(): lax.ppermute(lower, axis, upward)  5.18 us
  transfers between devices with their start and end apart: 9, of which 5 were waited for; matrix products, arithmetic and copies ran while one was open for 6% of the time, Pallas kernels for 0%

profile of v1, /device:TPU:0, one launch (start us, length us, event | category | flops | bytes accessed | tf_op | source)
XLA Modules:
  0.0 220.2 jit_solution(1654478903644720548)
XLA Ops:
  6.5 0.7 compare_select_fusion.4
  7.3 0.7 compare_and_fusion.1
  7.9 2.8 %gather_fusion = bf16[2,256,512]{2,1,0:T(8,128)(2,1)S(1)} fusion(bf16[16,256,512]{2,1,0:T(8,128)(2,1)} %param.8, s32[1024]{0:T(1024)S(1)} %pad_clamp_fusion.2), kind=kCustom, calls=%fused_computation | custom fusion | bytes 1048584 | tf_op jit(solution)/shard_map/jit(_take)/gather | solution.py:46
  10.8 3.0 %collective-permute-start = (bf16[2,256,512]{2,1,0:T(8,128)(2,1)S(1)}, bf16[2,256,512]{2,1,0:T(8,128)(2,1)S(1)}, u32[]{:S(2)}, u32[]{:S(2)}) collective-permute-start(bf16[2,256,512]{2,1,0:T(8,128)(2,1)S(1)} %broadcast_select_fusion), channel_id=1, source_target_pairs={{0,4},{4,8},{8,12},{12,16},{16,20},{20,24},{24,28},{28,0},{1,5},{5... | collective-permute-start | bytes 1572872 | tf_op jit(solution)/shard_map/ppermute | solution.py:11
  13.9 3.1 %collective-permute-start.1 = (bf16[2,256,512]{2,1,0:T(8,128)(2,1)S(1)}, bf16[2,256,512]{2,1,0:T(8,128)(2,1)S(1)}, u32[]{:S(2)}, u32[]{:S(2)}) collective-permute-start(bf16[2,256,512]{2,1,0:T(8,128)(2,1)S(1)} %broadcast_select_fusion), channel_id=1, source_target_pairs={{4,0},{8,4},{12,8},{16,12},{20,16},{24,20},{28,24},{0,28},{5,1},{9... | collective-permute-start | bytes 1572872 | tf_op jit(solution)/shard_map/ppermute | solution.py:11
  17.0 0.8 copy.81
  17.7 0.6 gather_fusion.1
  18.7 45.8 %all_gather.6 = bf16[16,64,192]{2,1,0:T(8,128)(2,1)S(1)} all-gather(bf16[2,64,192]{2,1,0:T(8,128)(2,1)} %param.6), channel_id=1, replica_groups=mesh['ka'=8,'col'=4] {'ka'}, dimensions={0}, use_global_device_ids=true | all-gather | bytes 442368 | tf_op jit(solution)/shard_map/all_gather | solution.py:37
  65.1 7.2 %all_gather.7 = bf16[4,256,192]{2,1,0:T(8,128)(2,1)S(1)} all-gather(bf16[4,64,192]{2,1,0:T(8,128)(2,1)S(1)} %broadcast_select_fusion.1), channel_id=1, replica_groups=mesh['ka'=8,'col'=4] {'col'}, dimensions={1}, use_global_device_ids=true | all-gather | bytes 491520 | tf_op jit(solution)/shard_map/all_gather | solution.py:39
  72.9 1.9 broadcast_in_dim.32
  74.8 1.2 convolution_dynamic-update-slice_fusion.7
  76.2 4.5 %collective-permute-start.3 = (bf16[2,256,512]{2,1,0:T(8,128)(2,1)S(1)}, bf16[2,256,512]{2,1,0:T(8,128)(2,1)S(1)}, u32[]{:S(2)}, u32[]{:S(2)}) collective-permute-start(bf16[2,256,512]{2,1,0:T(8,128)(2,1)S(1)} %collective-permute-done.1), channel_id=1, source_target_pairs={{4,0},{8,4},{12,8},{16,12},{20,16},{24,20},{28,24},{0,28},{5,1},{9... | collective-permute-start | bytes 1572872 | tf_op jit(solution)/shard_map/ppermute | solution.py:24
  80.7 1.2 convolution_dynamic-update-slice_fusion.6
  81.9 1.2 convolution_dynamic-update-slice_fusion.5
  83.1 16.1 %collective-permute-done.2 = bf16[2,256,512]{2,1,0:T(8,128)(2,1)S(1)} collective-permute-done((bf16[2,256,512]{2,1,0:T(8,128)(2,1)S(1)}, bf16[2,256,512]{2,1,0:T(8,128)(2,1)S(1)}, u32[]{:S(2)}, u32[]{:S(2)}) %collective-permute-start.2) | collective-permute-done | bytes 524320 | tf_op jit(solution)/shard_map/ppermute | solution.py:24
  99.2 2.5 %collective-permute-start.4 = (bf16[2,256,512]{2,1,0:T(8,128)(2,1)S(1)}, bf16[2,256,512]{2,1,0:T(8,128)(2,1)S(1)}, u32[]{:S(2)}, u32[]{:S(2)}) collective-permute-start(bf16[2,256,512]{2,1,0:T(8,128)(2,1)S(1)} %collective-permute-done.2), channel_id=1, source_target_pairs={{0,4},{4,8},{8,12},{12,16},{16,20},{20,24},{24,28},{28,0},{1,5},{5... | collective-permute-start | bytes 1572872 | tf_op jit(solution)/shard_map/ppermute | solution.py:24
  101.7 2.7 %collective-permute-start.5 = (bf16[2,256,512]{2,1,0:T(8,128)(2,1)S(1)}, bf16[2,256,512]{2,1,0:T(8,128)(2,1)S(1)}, u32[]{:S(2)}, u32[]{:S(2)}) collective-permute-start(bf16[2,256,512]{2,1,0:T(8,128)(2,1)S(1)} %collective-permute-done.3), channel_id=1, source_target_pairs={{4,0},{8,4},{12,8},{16,12},{20,16},{24,20},{28,24},{0,28},{5,1},{9... | collective-permute-start | bytes 1572872 | tf_op jit(solution)/shard_map/ppermute | solution.py:24
  104.4 1.2 convolution_dynamic-update-slice_fusion.4
  105.6 1.2 convolution_dynamic-update-slice_fusion.3
  106.8 17.1 %collective-permute-done.4 = bf16[2,256,512]{2,1,0:T(8,128)(2,1)S(1)} collective-permute-done((bf16[2,256,512]{2,1,0:T(8,128)(2,1)S(1)}, bf16[2,256,512]{2,1,0:T(8,128)(2,1)S(1)}, u32[]{:S(2)}, u32[]{:S(2)}) %collective-permute-start.4) | collective-permute-done | bytes 524320 | tf_op jit(solution)/shard_map/ppermute | solution.py:24
  123.8 2.5 %collective-permute-start.6 = (bf16[2,256,512]{2,1,0:T(8,128)(2,1)S(1)}, bf16[2,256,512]{2,1,0:T(8,128)(2,1)S(1)}, u32[]{:S(2)}, u32[]{:S(2)}) collective-permute-start(bf16[2,256,512]{2,1,0:T(8,128)(2,1)S(1)} %collective-permute-done.4), channel_id=1, source_target_pairs={{0,4},{4,8},{8,12},{12,16},{16,20},{20,24},{24,28},{28,0},{1,5},{5... | collective-permute-start | bytes 1572872 | tf_op jit(solution)/shard_map/ppermute | solution.py:24
  126.3 1.2 convolution_dynamic-update-slice_fusion.2
  127.5 1.2 convolution_dynamic-update-slice_fusion.1
  128.7 10.9 %collective-permute-done.6 = bf16[2,256,512]{2,1,0:T(8,128)(2,1)S(1)} collective-permute-done((bf16[2,256,512]{2,1,0:T(8,128)(2,1)S(1)}, bf16[2,256,512]{2,1,0:T(8,128)(2,1)S(1)}, u32[]{:S(2)}, u32[]{:S(2)}) %collective-permute-start.6) | collective-permute-done | bytes 524320 | tf_op jit(solution)/shard_map/ppermute | solution.py:24
  139.6 1.2 convolution_dynamic-update-slice_fusion
  140.9 35.8 %reduce-scatter.2.cloned.1.call-done = bf16[2,512,384]{2,1,0:T(8,128)(2,1)} async-done(((bf16[2,2048,384]{2,1,0:T(8,128)(2,1)}), bf16[2,512,384]{2,1,0:T(8,128)(2,1)}) %reduce-scatter.2.cloned.1.call-update) | async-done | bytes 786448 | tf_op jit(solution)/shard_map/reduce_scatter | solution.py:56
  176.7 1.2 convert_reduce_fusion
  178.4 0.9 copy.96
  179.3 0.6 dynamic-slice
  180.5 31.2 %all-reduce.3.cloned.1.call-done = bf16[2,256,192]{2,0,1:T(2,128)(2,1)} async-done(((bf16[2,256,192]{2,0,1:T(2,128)(2,1)}), bf16[2,256,192]{2,0,1:T(2,128)(2,1)}) %all-reduce.3.cloned.1.call-update) | async-done | bytes 196624
  211.7 0.9 constant_dynamic-slice_fusion
  212.6 0.7 multiply_add_fusion
  (34 shorter events, 2.5 us)
Async XLA Ops:
  6.5 65.8 %copy-start = (bf16[2,512,256]{2,1,0:T(8,128)(2,1)S(1)}, bf16[2,512,256]{2,1,0:T(8,128)(2,1)}, u32[]{:S(2)}) copy-start(bf16[2,512,256]{2,1,0:T(8,128)(2,1)} %param.7) | copy-start | bytes 1572868
  6.5 170.1 %reduce-scatter.2.cloned.1.call-start = ((), (), s32[]{:S(2)}) async-start(), calls=%async_computation.1 | async-start | bytes 3932160 | tf_op jit(solution)/shard_map/reduce_scatter | solution.py:56
  10.8 65.2 %collective-permute-start = (bf16[2,256,512]{2,1,0:T(8,128)(2,1)S(1)}, bf16[2,256,512]{2,1,0:T(8,128)(2,1)S(1)}, u32[]{:S(2)}, u32[]{:S(2)}) collective-permute-start(bf16[2,256,512]{2,1,0:T(8,128)(2,1)S(1)} %broadcast_select_fusion), channel_id=1, source_target_pairs={{0,4},{4,8},{8,12},{12,16},{16,20},{20,24},{24,28},{28,0},{1,5},{5... | collective-permute-start | bytes 1572872 | tf_op jit(solution)/shard_map/ppermute | solution.py:11
  13.9 62.4 %collective-permute-start.1 = (bf16[2,256,512]{2,1,0:T(8,128)(2,1)S(1)}, bf16[2,256,512]{2,1,0:T(8,128)(2,1)S(1)}, u32[]{:S(2)}, u32[]{:S(2)}) collective-permute-start(bf16[2,256,512]{2,1,0:T(8,128)(2,1)S(1)} %broadcast_select_fusion), channel_id=1, source_target_pairs={{4,0},{8,4},{12,8},{16,12},{20,16},{24,20},{28,24},{0,28},{5,1},{9... | collective-permute-start | bytes 1572872 | tf_op jit(solution)/shard_map/ppermute | solution.py:11
  76.0 23.2 %collective-permute-start.2 = (bf16[2,256,512]{2,1,0:T(8,128)(2,1)S(1)}, bf16[2,256,512]{2,1,0:T(8,128)(2,1)S(1)}, u32[]{:S(2)}, u32[]{:S(2)}) collective-permute-start(bf16[2,256,512]{2,1,0:T(8,128)(2,1)S(1)} %collective-permute-done), channel_id=1, source_target_pairs={{0,4},{4,8},{8,12},{12,16},{16,20},{20,24},{24,28},{28,0},{1,5},{5... | collective-permute-start | bytes 1572872 | tf_op jit(solution)/shard_map/ppermute | solution.py:24
  76.2 25.5 %collective-permute-start.3 = (bf16[2,256,512]{2,1,0:T(8,128)(2,1)S(1)}, bf16[2,256,512]{2,1,0:T(8,128)(2,1)S(1)}, u32[]{:S(2)}, u32[]{:S(2)}) collective-permute-start(bf16[2,256,512]{2,1,0:T(8,128)(2,1)S(1)} %collective-permute-done.1), channel_id=1, source_target_pairs={{4,0},{8,4},{12,8},{16,12},{20,16},{24,20},{28,24},{0,28},{5,1},{9... | collective-permute-start | bytes 1572872 | tf_op jit(solution)/shard_map/ppermute | solution.py:24
  99.2 24.6 %collective-permute-start.4 = (bf16[2,256,512]{2,1,0:T(8,128)(2,1)S(1)}, bf16[2,256,512]{2,1,0:T(8,128)(2,1)S(1)}, u32[]{:S(2)}, u32[]{:S(2)}) collective-permute-start(bf16[2,256,512]{2,1,0:T(8,128)(2,1)S(1)} %collective-permute-done.2), channel_id=1, source_target_pairs={{0,4},{4,8},{8,12},{12,16},{16,20},{20,24},{24,28},{28,0},{1,5},{5... | collective-permute-start | bytes 1572872 | tf_op jit(solution)/shard_map/ppermute | solution.py:24
  101.7 25.8 %collective-permute-start.5 = (bf16[2,256,512]{2,1,0:T(8,128)(2,1)S(1)}, bf16[2,256,512]{2,1,0:T(8,128)(2,1)S(1)}, u32[]{:S(2)}, u32[]{:S(2)}) collective-permute-start(bf16[2,256,512]{2,1,0:T(8,128)(2,1)S(1)} %collective-permute-done.3), channel_id=1, source_target_pairs={{4,0},{8,4},{12,8},{16,12},{20,16},{24,20},{28,24},{0,28},{5,1},{9... | collective-permute-start | bytes 1572872 | tf_op jit(solution)/shard_map/ppermute | solution.py:24
  123.8 15.8 %collective-permute-start.6 = (bf16[2,256,512]{2,1,0:T(8,128)(2,1)S(1)}, bf16[2,256,512]{2,1,0:T(8,128)(2,1)S(1)}, u32[]{:S(2)}, u32[]{:S(2)}) collective-permute-start(bf16[2,256,512]{2,1,0:T(8,128)(2,1)S(1)} %collective-permute-done.4), channel_id=1, source_target_pairs={{0,4},{4,8},{8,12},{12,16},{16,20},{20,24},{24,28},{28,0},{1,5},{5... | collective-permute-start | bytes 1572872 | tf_op jit(solution)/shard_map/ppermute | solution.py:24
  140.8 38.5 %copy-start.3 = (u32[32]{0:T(128)S(1)}, u32[32]{0:T(128)}, u32[]{:S(2)}) copy-start(u32[32]{0:T(128)} %constant.111) | copy-start | bytes 388
  140.8 71.8 %copy-start.1 = (bf16[2,64,192]{2,1,0:T(8,128)(2,1)S(1)}, bf16[2,64,192]{2,1,0:T(8,128)(2,1)}, u32[]{:S(2)}) copy-start(bf16[2,64,192]{2,1,0:T(8,128)(2,1)} %param.6) | copy-start | bytes 147460
  140.8 71.8 %copy-start.2 = (f32[2,64]{1,0:T(2,128)S(1)}, f32[2,64]{1,0:T(2,128)}, u32[]{:S(2)}) copy-start(f32[2,64]{1,0:T(2,128)} %param.9) | copy-start | bytes 1540
  140.9 70.8 %all-reduce.3.cloned.1.call-start = ((), (), s32[]{:S(2)}) async-start(), calls=%async_computation.2 | async-start | bytes 524288
Sparse Core Ops, SparseCore 0:
  141.0 35.6 reduce-scatter.1
  179.4 32.2 all-reduce.2
